TPU v7x, 256 devices: a whole 4x4x8 slice. The times are simulated.
256 devices in a mesh: section: 4 (over x_hi, core), tp: 2 (over x_lo), doc: 32 (over z, y).
Axes of the slice: x: 4 (x_hi: 2, x_lo: 2; x = x_hi * 2 + x_lo), y: 4, z: 8, core: 2. Of those that a mesh axis runs over, the one named last changes fastest.
Arguments:
- token_ids: int32 [64, 2, 32], P('doc'), may hold values from 0 to 16383
- seg_lengths: int32 [64, 2], P('doc'), may hold values from 1 to 32
- emb_table: bfloat16 [16384, 4096], P('section', 'tp'), may hold values from -6 to 6
- mem_init: bfloat16 [16, 4096], P(None, 'tp'), may hold values from -6 to 6
- norm_gain: float32 [4, 4096], P('section'), may hold values from 0.1 to 1.9
- w_query: bfloat16 [4, 4096, 2048], P('section', 'doc', 'tp'), may hold values from -0.09375 to 0.09375
- w_key: bfloat16 [4, 4096, 2048], P('section', 'doc', 'tp'), may hold values from -0.09375 to 0.09375
- w_value: bfloat16 [4, 4096, 2048], P('section', 'doc', 'tp'), may hold values from -0.09375 to 0.09375
- w_out: bfloat16 [4, 2048, 4096], P('section', None, 'tp'), may hold values from -0.125 to 0.125
- layer_mix: float32 [4], P('section'), may hold values from 0.5 to 4.5
Outputs:
- pooled: float32 [64, 4096], P(None, 'tp')
All inputs are finite; a program needn't handle non-finite values.
Results may differ from a plain program's by a relative error of at most 0.013.
Values may be sent and summed in bfloat16 or wider, within the bound.
A program may use at most 192 MiB of HBM per device.

v0:
```python
import math
import jax
import jax.numpy as jnp
from jax import lax
from jax.sharding import PartitionSpec as P

HD = 128
M = 16
L = 32
SEGS = 2
EPSILON = 1e-05
NEGATIVE = -1e30


def side_by_side(arrays, axis, dim, along):
    widths = [a.shape[along] for a in arrays]
    both = jnp.concatenate(arrays, axis=along)
    out = lax.all_gather(both, axis, axis=dim, tiled=True)
    return tuple(jnp.split(out, [sum(widths[:k]) for k in range(1, len(widths))], axis=along))


def from_behind(block, axis, distance):
    devices = range(lax.axis_size(axis))
    route = [((i - distance) % len(devices), i) for i in devices]
    return lax.ppermute(block, axis, route)


def laid_out(parts, dim):
    lengths = list(parts.shape[1:])
    lengths[dim] *= parts.shape[0]
    return jnp.moveaxis(parts, 0, dim).reshape(lengths)


def copy_for_each(shard, axis):
    copies = jnp.broadcast_to(shard, (lax.axis_size(axis), *shard.shape))
    return lax.all_to_all(copies, axis, split_axis=0, concat_axis=0, tiled=True)


def collect(shard, axis, dim):
    return laid_out(copy_for_each(shard, axis), dim)


def visible_rows(row_count, length):
    position = jnp.arange(row_count)
    key_ok = (position < M) | (position - M < length)
    ordered = (
        (position[None, :] < M) | (position[:, None] < M) | (position[None, :] <= position[:, None])
    )
    return key_ok[None, :] & ordered


def attend(features, length, query_proj, key_proj, value_proj, norm_row):
    row_count = features.shape[0]
    local_heads = query_proj.shape[1] // HD
    floats = features.astype(jnp.float32)
    mean_square = jnp.mean(floats * floats, -1, keepdims=True)
    normed = (floats * lax.rsqrt(mean_square + EPSILON) * norm_row).astype(jnp.bfloat16)
    head_shape = (row_count, local_heads, HD)
    queries = (
        jnp.dot(normed, query_proj, preferred_element_type=jnp.float32)
        .astype(jnp.bfloat16)
        .reshape(head_shape)
    )
    keys = (
        jnp.dot(normed, key_proj, preferred_element_type=jnp.float32)
        .astype(jnp.bfloat16)
        .reshape(head_shape)
    )
    values = (
        jnp.dot(normed, value_proj, preferred_element_type=jnp.float32)
        .astype(jnp.bfloat16)
        .reshape(head_shape)
    )
    scores = jnp.einsum("qhe,khe->hqk", queries, keys, preferred_element_type=jnp.float32) * (
        1.0 / math.sqrt(HD)
    )
    allowed = visible_rows(row_count, length)[None]
    scores = jnp.where(allowed, scores, NEGATIVE)
    weights = jnp.where(allowed, jnp.exp(scores), 0.0)
    probs = (weights / jnp.sum(weights, -1, keepdims=True)).astype(jnp.bfloat16)
    mixed = jnp.einsum("hqk,khe->qhe", probs, values, preferred_element_type=jnp.float32).astype(
        jnp.bfloat16
    )
    return mixed.reshape(row_count, local_heads * HD)


def body(
    token_ids,
    seg_lengths,
    emb_table,
    mem_init,
    norm_gain,
    w_query,
    w_key,
    w_value,
    w_out,
    layer_mix,
):
    phases = lax.axis_size("section")
    phase_index = lax.axis_index("section")
    doc_local = token_ids.shape[0]
    vocab_rows = emb_table.shape[0]
    width_local = emb_table.shape[1]
    flat_ids = token_ids.reshape(-1)
    local_ids = flat_ids - phase_index * vocab_rows
    owned = (local_ids >= 0) & (local_ids < vocab_rows)
    picked_rows = jnp.take(emb_table, jnp.clip(local_ids, 0, vocab_rows - 1), axis=0)
    partial_rows = jnp.where(owned[:, None], picked_rows.astype(jnp.float32), 0.0)
    embedded = lax.psum(partial_rows.astype(jnp.bfloat16), "section")
    embedded = embedded.reshape(doc_local * SEGS, L, width_local)
    query_proj, key_proj, value_proj = side_by_side((w_query[0], w_key[0], w_value[0]), "doc", 0, 1)
    out_proj = w_out[0]
    norm_row = norm_gain[0]
    mixing = layer_mix[0]
    row_count = M + L
    head_cols = query_proj.shape[1]
    total_turns = (SEGS - 1) * phases + doc_local + phases - 1

    def turn(turn_index, carried):
        incoming, returned, pooled = carried
        offset = turn_index - phase_index
        segment = offset // phases
        document = offset % phases
        active = (offset >= 0) & (document < doc_local) & (segment < SEGS)
        segment = jnp.clip(segment, 0, SEGS - 1)
        document = jnp.clip(document, 0, doc_local - 1)
        tokens = lax.dynamic_index_in_dim(embedded, document * SEGS + segment, 0, keepdims=False)
        earlier = incoming[:M]
        memory = jnp.where(segment == 0, mem_init, earlier)
        hidden = jnp.where(phase_index == 0, jnp.concatenate([memory, tokens], 0), incoming)
        length = seg_lengths[document, segment]
        features = lax.all_gather(hidden, "tp", axis=1, tiled=True)
        heads_out = lax.cond(
            active,
            lambda: attend(features, length, query_proj, key_proj, value_proj, norm_row),
            lambda: jnp.zeros((row_count, head_cols), jnp.bfloat16),
        )
        every_head = lax.all_gather(heads_out, "tp", axis=1, tiled=True)
        update = lax.cond(
            active,
            lambda: jnp.dot(every_head, out_proj, preferred_element_type=jnp.float32),
            lambda: jnp.zeros((row_count, width_local), jnp.float32),
        )
        result = (hidden.astype(jnp.float32) + update).astype(jnp.bfloat16)
        token_ok = jnp.arange(L) < length
        summed = jnp.sum(
            jnp.where(token_ok[:, None], result[M:].astype(jnp.float32), 0.0), 0
        ) / length.astype(jnp.float32)
        scale_now = jnp.where(active & (segment == SEGS - 1), mixing, 0.0)
        picked = (jnp.arange(doc_local) == document).astype(jnp.float32)
        pooled = pooled + picked[:, None] * (scale_now * summed)[None, :]
        incoming = from_behind(result, "section", 1)
        return (incoming, returned, pooled)

    start_state = (
        jnp.zeros((row_count, width_local), jnp.bfloat16),
        jnp.zeros((M, width_local), jnp.bfloat16),
        jnp.zeros((doc_local, width_local), jnp.float32),
    )
    final_state = lax.fori_loop(0, total_turns, turn, start_state)
    pooled = final_state[2]
    layer_total = lax.psum(pooled, "section")
    return collect(layer_total, "doc", 0)


def solution(mesh):
    return jax.shard_map(
        body,
        mesh=mesh,
        in_specs=(
            P("doc", None, None),
            P("doc", None),
            P("section", "tp"),
            P(None, "tp"),
            P("section", None),
            P("section", "doc", "tp"),
            P("section", "doc", "tp"),
            P("section", "doc", "tp"),
            P("section", None, "tp"),
            P("section"),
        ),
        out_specs=P(None, "tp"),
        check_vma=False,
    )
```

profile of v0, /device:TPU:6, one launch (start us, length us, event | category | flops | bytes accessed | tf_op | source)
XLA Modules:
  0.0 544.1 jit_solution(7246789136166503386)
XLA Ops:
  7.4 2.1 pad_maximum_fusion
  11.2 9.4 %gather_fusion = bf16[128,2048]{1,0:T(8,128)(2,1)S(1)} fusion(bf16[4096,2048]{1,0:T(8,128)(2,1)} %param.18, s32[1024]{0:T(1024)S(1)} %pad_clamp_fusion), kind=kCustom, calls=%fused_computation | custom fusion | bytes 1049088 | tf_op jit(solution)/shard_map/jit(_take)/gather | solution.py:107
  20.6 1.1 select_convert_fusion
  21.8 175.4 %all-gather.2.cloned.1.call-done = bf16[4096,3072]{1,0:T(8,128)(2,1)} async-done(((bf16[128,3072]{1,0:T(8,128)(2,1)}), bf16[4096,3072]{1,0:T(8,128)(2,1)}) %all-gather.2.cloned.1.call-update) | async-done | bytes 25165840 | tf_op jit(solution)/shard_map/all_gather | solution.py:18
  197.2 16.9 %fusion.25 = (bf16[4096,1024]{1,0:T(8,128)(2,1)}, bf16[4096,1024]{1,0:T(8,128)(2,1)}, bf16[4096,1024]{1,0:T(8,128)(2,1)}) fusion(bf16[4096,3072]{1,0:T(8,128)(2,1)} %all-gather.2.cloned.1.call-done), kind=kLoop, calls=%fused_computation.52 | loop fusion | bytes 50331648 | tf_op jit(solution)/shard_map/split | solution.py:19
  214.2 284.0 %while.18 = (s32[]{:T(128)}, bf16[48,2048]{1,0:T(8,128)(2,1)S(1)}, f32[2,2048]{1,0:T(2,128)S(1)}, pred[]{:T(512)}, s32[]{:T(128)}, /*index=5*/bf16[16,2048]{1,0:...) while((s32[]{:T(128)}, bf16[48,2048]{1,0:T(8,128)(2,1)S(1)}, ...), condition=%wide.region_9.10_spmd.clone, body=%wide.region_1.9_spmd.clone.sunk | while | flops 1624327808 | bytes 90839752 | solution.py:160
  214.2 0.9 dynamic-slice_bitcast_fusion.2
  215.2 6.6 %all_gather.28 = bf16[48,4096]{1,0:T(8,128)(2,1)S(1)} all-gather(bf16[48,2048]{1,0:T(8,128)(2,1)S(1)} %maximum_select_fusion.2), channel_id=1, replica_groups=mesh['section'=4,'tp'=2,'doc'=32] {'tp'}, dimensions={1}, use_global_device_ids=true | all-gather | bytes 589824 | tf_op jit(solution)/shard_map/while/body/eval_jaxpr/all_gather | solution.py:132
  222.4 5.3 all_gather.29
  230.1 4.4 collective-permute-done
  234.5 0.9 dynamic-slice_bitcast_fusion.2
  235.5 6.3 %all_gather.28 = bf16[48,4096]{1,0:T(8,128)(2,1)S(1)} all-gather(bf16[48,2048]{1,0:T(8,128)(2,1)S(1)} %maximum_select_fusion.2), channel_id=1, replica_groups=mesh['section'=4,'tp'=2,'doc'=32] {'tp'}, dimensions={1}, use_global_device_ids=true | all-gather | bytes 589824 | tf_op jit(solution)/shard_map/while/body/eval_jaxpr/all_gather | solution.py:132
  242.5 6.3 %all_gather.29 = bf16[48,2048]{1,0:T(8,128)(2,1)S(1)} all-gather(bf16[48,1024]{1,0:T(8,128)(2,1)S(1)} %get-tuple-element.593), channel_id=1, replica_groups=mesh['section'=4,'tp'=2,'doc'=32] {'tp'}, dimensions={1}, use_global_device_ids=true | all-gather | bytes 294912 | tf_op jit(solution)/shard_map/while/body/eval_jaxpr/all_gather | solution.py:138
  248.8 10.6 %collective-permute-start = (bf16[48,2048]{1,0:T(8,128)(2,1)S(1)}, bf16[48,2048]{1,0:T(8,128)(2,1)S(1)}, u32[]{:S(2)}, u32[]{:S(2)}) collective-permute-start(bf16[48,2048]{1,0:T(8,128)(2,1)S(1)} %add_convert_fusion.2), channel_id=1, source_target_pairs={{192,0},{0,64},{64,128},{128,192},{193,1},{1,65},{65,129},{129,193... | collective-permute-start | bytes 589832 | tf_op jit(solution)/shard_map/while/body/eval_jaxpr/ppermute | solution.py:25
  261.6 15.0 %collective-permute-done = bf16[48,2048]{1,0:T(8,128)(2,1)S(1)} collective-permute-done((bf16[48,2048]{1,0:T(8,128)(2,1)S(1)}, bf16[48,2048]{1,0:T(8,128)(2,1)S(1)}, u32[]{:S(2)}, u32[]{:S(2)}) %collective-permute-start) | collective-permute-done | bytes 196640 | tf_op jit(solution)/shard_map/while/body/eval_jaxpr/ppermute | solution.py:25
  277.6 7.2 %all_gather.28 = bf16[48,4096]{1,0:T(8,128)(2,1)S(1)} all-gather(bf16[48,2048]{1,0:T(8,128)(2,1)S(1)} %maximum_select_fusion.2), channel_id=1, replica_groups=mesh['section'=4,'tp'=2,'doc'=32] {'tp'}, dimensions={1}, use_global_device_ids=true | all-gather | bytes 589824 | tf_op jit(solution)/shard_map/while/body/eval_jaxpr/all_gather | solution.py:132
  285.4 10.4 %conditional.6 = (bf16[48,1024]{1,0:T(8,128)(2,1)S(1)}) conditional(s32[]{:T(128)} %convert_element_type.148, () %tuple.64, (bf16[48,4096]{1,0:T(8,128)(2,1)S(1)}, f32[1,4096]{1,0:T(1,128)S(1)}, bf16[4096,1024]{1,0:T(8,128)(2,1)}, s32[]{:T(128)}, bf16[4096,1024]{1,0:T(8,128)(2,1)}, /*index=5*/bf16[4096,1024]{1,0:T(8,128)(2,1)}) %tuple.65), branch_computations={%region_2.2_spmd, %region_3.5_spmd} | conditional | flops 1220644480 | bytes 78157736 | solution.py:133
  285.7 5.2 fusion.5
  291.3 1.6 fusion.6
  294.0 1.6 fusion.4
  295.9 5.3 all_gather.29
  301.2 4.9 conditional.7
  301.2 4.9 fusion.26
  308.4 4.4 collective-permute-done
  313.9 6.3 %all_gather.28 = bf16[48,4096]{1,0:T(8,128)(2,1)S(1)} all-gather(bf16[48,2048]{1,0:T(8,128)(2,1)S(1)} %maximum_select_fusion.2), channel_id=1, replica_groups=mesh['section'=4,'tp'=2,'doc'=32] {'tp'}, dimensions={1}, use_global_device_ids=true | all-gather | bytes 589824 | tf_op jit(solution)/shard_map/while/body/eval_jaxpr/all_gather | solution.py:132
  320.8 10.4 %conditional.6 = (bf16[48,1024]{1,0:T(8,128)(2,1)S(1)}) conditional(s32[]{:T(128)} %convert_element_type.148, () %tuple.64, (bf16[48,4096]{1,0:T(8,128)(2,1)S(1)}, f32[1,4096]{1,0:T(1,128)S(1)}, bf16[4096,1024]{1,0:T(8,128)(2,1)}, s32[]{:T(128)}, bf16[4096,1024]{1,0:T(8,128)(2,1)}, /*index=5*/bf16[4096,1024]{1,0:T(8,128)(2,1)}) %tuple.65), branch_computations={%region_2.2_spmd, %region_3.5_spmd} | conditional | flops 1220644480 | bytes 78157736 | solution.py:133
  321.0 5.2 fusion.5
  326.7 1.6 fusion.6
  329.3 1.6 fusion.4
  331.3 6.3 %all_gather.29 = bf16[48,2048]{1,0:T(8,128)(2,1)S(1)} all-gather(bf16[48,1024]{1,0:T(8,128)(2,1)S(1)} %get-tuple-element.593), channel_id=1, replica_groups=mesh['section'=4,'tp'=2,'doc'=32] {'tp'}, dimensions={1}, use_global_device_ids=true | all-gather | bytes 294912 | tf_op jit(solution)/shard_map/while/body/eval_jaxpr/all_gather | solution.py:138
  337.6 4.9 conditional.7
  337.6 4.9 fusion.26
  344.8 5.1 collective-permute-done
  351.0 6.3 %all_gather.28 = bf16[48,4096]{1,0:T(8,128)(2,1)S(1)} all-gather(bf16[48,2048]{1,0:T(8,128)(2,1)S(1)} %maximum_select_fusion.2), channel_id=1, replica_groups=mesh['section'=4,'tp'=2,'doc'=32] {'tp'}, dimensions={1}, use_global_device_ids=true | all-gather | bytes 589824 | tf_op jit(solution)/shard_map/while/body/eval_jaxpr/all_gather | solution.py:132
  357.9 5.3 all_gather.29
  363.3 7.2 %collective-permute-start = (bf16[48,2048]{1,0:T(8,128)(2,1)S(1)}, bf16[48,2048]{1,0:T(8,128)(2,1)S(1)}, u32[]{:S(2)}, u32[]{:S(2)}) collective-permute-start(bf16[48,2048]{1,0:T(8,128)(2,1)S(1)} %add_convert_fusion.2), channel_id=1, source_target_pairs={{192,0},{0,64},{64,128},{128,192},{193,1},{1,65},{65,129},{129,193... | collective-permute-start | bytes 589832 | tf_op jit(solution)/shard_map/while/body/eval_jaxpr/ppermute | solution.py:25
  372.8 0.9 dynamic-slice_bitcast_fusion.2
  373.8 7.8 %all_gather.28 = bf16[48,4096]{1,0:T(8,128)(2,1)S(1)} all-gather(bf16[48,2048]{1,0:T(8,128)(2,1)S(1)} %maximum_select_fusion.2), channel_id=1, replica_groups=mesh['section'=4,'tp'=2,'doc'=32] {'tp'}, dimensions={1}, use_global_device_ids=true | all-gather | bytes 589824 | tf_op jit(solution)/shard_map/while/body/eval_jaxpr/all_gather | solution.py:132
  382.3 5.3 all_gather.29
  389.9 12.3 %collective-permute-done = bf16[48,2048]{1,0:T(8,128)(2,1)S(1)} collective-permute-done((bf16[48,2048]{1,0:T(8,128)(2,1)S(1)}, bf16[48,2048]{1,0:T(8,128)(2,1)S(1)}, u32[]{:S(2)}, u32[]{:S(2)}) %collective-permute-start) | collective-permute-done | bytes 196640 | tf_op jit(solution)/shard_map/while/body/eval_jaxpr/ppermute | solution.py:25
  403.2 7.1 %all_gather.28 = bf16[48,4096]{1,0:T(8,128)(2,1)S(1)} all-gather(bf16[48,2048]{1,0:T(8,128)(2,1)S(1)} %maximum_select_fusion.2), channel_id=1, replica_groups=mesh['section'=4,'tp'=2,'doc'=32] {'tp'}, dimensions={1}, use_global_device_ids=true | all-gather | bytes 589824 | tf_op jit(solution)/shard_map/while/body/eval_jaxpr/all_gather | solution.py:132
  410.9 10.4 %conditional.6 = (bf16[48,1024]{1,0:T(8,128)(2,1)S(1)}) conditional(s32[]{:T(128)} %convert_element_type.148, () %tuple.64, (bf16[48,4096]{1,0:T(8,128)(2,1)S(1)}, f32[1,4096]{1,0:T(1,128)S(1)}, bf16[4096,1024]{1,0:T(8,128)(2,1)}, s32[]{:T(128)}, bf16[4096,1024]{1,0:T(8,128)(2,1)}, /*index=5*/bf16[4096,1024]{1,0:T(8,128)(2,1)}) %tuple.65), branch_computations={%region_2.2_spmd, %region_3.5_spmd} | conditional | flops 1220644480 | bytes 78157736 | solution.py:133
  411.1 5.2 fusion.5
  416.8 1.6 fusion.6
  419.4 1.6 fusion.4
  421.3 5.3 all_gather.29
  426.6 4.9 conditional.7
  426.6 4.9 fusion.26
  433.9 4.4 collective-permute-done
  439.3 6.3 %all_gather.28 = bf16[48,4096]{1,0:T(8,128)(2,1)S(1)} all-gather(bf16[48,2048]{1,0:T(8,128)(2,1)S(1)} %maximum_select_fusion.2), channel_id=1, replica_groups=mesh['section'=4,'tp'=2,'doc'=32] {'tp'}, dimensions={1}, use_global_device_ids=true | all-gather | bytes 589824 | tf_op jit(solution)/shard_map/while/body/eval_jaxpr/all_gather | solution.py:132
  446.2 10.4 %conditional.6 = (bf16[48,1024]{1,0:T(8,128)(2,1)S(1)}) conditional(s32[]{:T(128)} %convert_element_type.148, () %tuple.64, (bf16[48,4096]{1,0:T(8,128)(2,1)S(1)}, f32[1,4096]{1,0:T(1,128)S(1)}, bf16[4096,1024]{1,0:T(8,128)(2,1)}, s32[]{:T(128)}, bf16[4096,1024]{1,0:T(8,128)(2,1)}, /*index=5*/bf16[4096,1024]{1,0:T(8,128)(2,1)}) %tuple.65), branch_computations={%region_2.2_spmd, %region_3.5_spmd} | conditional | flops 1220644480 | bytes 78157736 | solution.py:133
  446.4 5.2 fusion.5
  452.1 1.6 fusion.6
  454.7 1.6 fusion.4
  456.7 6.3 %all_gather.29 = bf16[48,2048]{1,0:T(8,128)(2,1)S(1)} all-gather(bf16[48,1024]{1,0:T(8,128)(2,1)S(1)} %get-tuple-element.593), channel_id=1, replica_groups=mesh['section'=4,'tp'=2,'doc'=32] {'tp'}, dimensions={1}, use_global_device_ids=true | all-gather | bytes 294912 | tf_op jit(solution)/shard_map/while/body/eval_jaxpr/all_gather | solution.py:138
  463.0 4.9 conditional.7
  463.0 4.9 fusion.26
  470.3 5.1 collective-permute-done
  476.4 6.3 %all_gather.28 = bf16[48,4096]{1,0:T(8,128)(2,1)S(1)} all-gather(bf16[48,2048]{1,0:T(8,128)(2,1)S(1)} %maximum_select_fusion.2), channel_id=1, replica_groups=mesh['section'=4,'tp'=2,'doc'=32] {'tp'}, dimensions={1}, use_global_device_ids=true | all-gather | bytes 589824 | tf_op jit(solution)/shard_map/while/body/eval_jaxpr/all_gather | solution.py:132
  483.4 5.3 all_gather.29
  488.7 7.2 %collective-permute-start = (bf16[48,2048]{1,0:T(8,128)(2,1)S(1)}, bf16[48,2048]{1,0:T(8,128)(2,1)S(1)}, u32[]{:S(2)}, u32[]{:S(2)}) collective-permute-start(bf16[48,2048]{1,0:T(8,128)(2,1)S(1)} %add_convert_fusion.2), channel_id=1, source_target_pairs={{192,0},{0,64},{64,128},{128,192},{193,1},{1,65},{65,129},{129,193... | collective-permute-start | bytes 589832 | tf_op jit(solution)/shard_map/while/body/eval_jaxpr/ppermute | solution.py:25
  498.2 13.7 %psum.15 = f32[2,2048]{1,0:T(2,128)S(1)} all-reduce(f32[2,2048]{1,0:T(2,128)S(1)} %get-tuple-element.366), channel_id=1, replica_groups=mesh['section'=4,'tp'=2,'doc'=32] {'section'}, use_global_device_ids=true, to_apply=%region_10.11 | all-reduce | flops 4096 | bytes 32768 | tf_op jit(solution)/shard_map/psum | solution.py:162
  512.1 23.4 %all_to_all.5 = f32[32,2,2048]{2,1,0:T(2,128)S(1)} all-to-all(f32[32,2,2048]{2,1,0:T(2,128)S(1)} %broadcast_in_dim.106), channel_id=1, replica_groups=mesh['section'=4,'tp'=2,'doc'=32] {'doc'}, dimensions={0} | all-to-all | bytes 1048576 | tf_op jit(solution)/shard_map/all_to_all | solution.py:36
  535.5 1.2 reshape.165
  (205 shorter events, 29.9 us)
Async XLA Ops:
  7.4 189.8 %all-gather.2.cloned.1.call-start = ((), (), s32[]{:S(2)}) async-start(), calls=%async_computation.2 | async-start | bytes 25952256 | tf_op jit(solution)/shard_map/all_gather | solution.py:18
  9.5 204.6 %all-reduce.2.cloned.1.call-start = ((), (), s32[]{:S(2)}) async-start(), calls=%async_computation.1 | async-start | bytes 1048576 | tf_op jit(solution)/shard_map/psum | solution.py:109
  21.7 192.4 %copy-start = (f32[1,4096]{1,0:T(1,128)S(1)}, f32[1,4096]{1,0:T(1,128)}, u32[]{:S(2)}) copy-start(f32[1,4096]{1,0:T(1,128)} %param.20) | copy-start | bytes 49156
  21.7 192.4 %copy-start.1 = (bf16[16,2048]{1,0:T(8,128)(2,1)S(1)}, bf16[16,2048]{1,0:T(8,128)(2,1)}, u32[]{:S(2)}) copy-start(bf16[16,2048]{1,0:T(8,128)(2,1)} %param.19) | copy-start | bytes 196612
  21.8 192.4 %copy-start.2 = (s32[2,2]{1,0:T(2,128)S(1)}, s32[2,2]{1,0:T(2,128)}, u32[]{:S(2)}) copy-start(s32[2,2]{1,0:T(2,128)} %param.17) | copy-start | bytes 52
  227.8 6.7 %collective-permute-start = (bf16[48,2048]{1,0:T(8,128)(2,1)S(1)}, bf16[48,2048]{1,0:T(8,128)(2,1)S(1)}, u32[]{:S(2)}, u32[]{:S(2)}) collective-permute-start(bf16[48,2048]{1,0:T(8,128)(2,1)S(1)} %add_convert_fusion.2), channel_id=1, source_target_pairs={{192,0},{0,64},{64,128},{128,192},{193,1},{1,65},{65,129},{129,193... | collective-permute-start | bytes 589832 | tf_op jit(solution)/shard_map/while/body/eval_jaxpr/ppermute | solution.py:25
  248.8 27.7 %collective-permute-start = (bf16[48,2048]{1,0:T(8,128)(2,1)S(1)}, bf16[48,2048]{1,0:T(8,128)(2,1)S(1)}, u32[]{:S(2)}, u32[]{:S(2)}) collective-permute-start(bf16[48,2048]{1,0:T(8,128)(2,1)S(1)} %add_convert_fusion.2), channel_id=1, source_target_pairs={{192,0},{0,64},{64,128},{128,192},{193,1},{1,65},{65,129},{129,193... | collective-permute-start | bytes 589832 | tf_op jit(solution)/shard_map/while/body/eval_jaxpr/ppermute | solution.py:25
  285.4 5.4 slice-start
  285.6 5.7 %slice-start.1 = ((s8[8388608]{0:T(1024)(128)(4,1)}), s8[4194304]{0:T(1024)(128)(4,1)S(1)}, s32[]{:S(2)}) async-start(s8[8388608]{0:T(1024)(128)(4,1)} %bitcast.43), calls=%async_computation.4 | async-start | bytes 8388608 | tf_op jit(solution)/shard_map/while/body/eval_jaxpr/cond
  285.6 8.3 %slice-start.2 = ((s8[8388608]{0:T(1024)(128)(4,1)}), s8[4194304]{0:T(1024)(128)(4,1)S(1)}, s32[]{:S(2)}) async-start(s8[8388608]{0:T(1024)(128)(4,1)} %bitcast.45), calls=%async_computation.5 | async-start | bytes 8388608 | tf_op jit(solution)/shard_map/while/body/eval_jaxpr/cond
  291.3 2.6 slice-start.3
  306.2 6.7 %collective-permute-start = (bf16[48,2048]{1,0:T(8,128)(2,1)S(1)}, bf16[48,2048]{1,0:T(8,128)(2,1)S(1)}, u32[]{:S(2)}, u32[]{:S(2)}) collective-permute-start(bf16[48,2048]{1,0:T(8,128)(2,1)S(1)} %add_convert_fusion.2), channel_id=1, source_target_pairs={{192,0},{0,64},{64,128},{128,192},{193,1},{1,65},{65,129},{129,193... | collective-permute-start | bytes 589832 | tf_op jit(solution)/shard_map/while/body/eval_jaxpr/ppermute | solution.py:25
  320.8 5.4 slice-start
  321.0 5.7 %slice-start.1 = ((s8[8388608]{0:T(1024)(128)(4,1)}), s8[4194304]{0:T(1024)(128)(4,1)S(1)}, s32[]{:S(2)}) async-start(s8[8388608]{0:T(1024)(128)(4,1)} %bitcast.43), calls=%async_computation.4 | async-start | bytes 8388608 | tf_op jit(solution)/shard_map/while/body/eval_jaxpr/cond
  321.0 8.3 %slice-start.2 = ((s8[8388608]{0:T(1024)(128)(4,1)}), s8[4194304]{0:T(1024)(128)(4,1)S(1)}, s32[]{:S(2)}) async-start(s8[8388608]{0:T(1024)(128)(4,1)} %bitcast.45), calls=%async_computation.5 | async-start | bytes 8388608 | tf_op jit(solution)/shard_map/while/body/eval_jaxpr/cond
  326.7 2.6 slice-start.3
  342.6 7.4 %collective-permute-start = (bf16[48,2048]{1,0:T(8,128)(2,1)S(1)}, bf16[48,2048]{1,0:T(8,128)(2,1)S(1)}, u32[]{:S(2)}, u32[]{:S(2)}) collective-permute-start(bf16[48,2048]{1,0:T(8,128)(2,1)S(1)} %add_convert_fusion.2), channel_id=1, source_target_pairs={{192,0},{0,64},{64,128},{128,192},{193,1},{1,65},{65,129},{129,193... | collective-permute-start | bytes 589832 | tf_op jit(solution)/shard_map/while/body/eval_jaxpr/ppermute | solution.py:25
  363.3 9.4 %collective-permute-start = (bf16[48,2048]{1,0:T(8,128)(2,1)S(1)}, bf16[48,2048]{1,0:T(8,128)(2,1)S(1)}, u32[]{:S(2)}, u32[]{:S(2)}) collective-permute-start(bf16[48,2048]{1,0:T(8,128)(2,1)S(1)} %add_convert_fusion.2), channel_id=1, source_target_pairs={{192,0},{0,64},{64,128},{128,192},{193,1},{1,65},{65,129},{129,193... | collective-permute-start | bytes 589832 | tf_op jit(solution)/shard_map/while/body/eval_jaxpr/ppermute | solution.py:25
  387.6 14.6 %collective-permute-start = (bf16[48,2048]{1,0:T(8,128)(2,1)S(1)}, bf16[48,2048]{1,0:T(8,128)(2,1)S(1)}, u32[]{:S(2)}, u32[]{:S(2)}) collective-permute-start(bf16[48,2048]{1,0:T(8,128)(2,1)S(1)} %add_convert_fusion.2), channel_id=1, source_target_pairs={{192,0},{0,64},{64,128},{128,192},{193,1},{1,65},{65,129},{129,193... | collective-permute-start | bytes 589832 | tf_op jit(solution)/shard_map/while/body/eval_jaxpr/ppermute | solution.py:25
  410.9 5.4 slice-start
  411.1 5.7 %slice-start.1 = ((s8[8388608]{0:T(1024)(128)(4,1)}), s8[4194304]{0:T(1024)(128)(4,1)S(1)}, s32[]{:S(2)}) async-start(s8[8388608]{0:T(1024)(128)(4,1)} %bitcast.43), calls=%async_computation.4 | async-start | bytes 8388608 | tf_op jit(solution)/shard_map/while/body/eval_jaxpr/cond
  411.1 8.3 %slice-start.2 = ((s8[8388608]{0:T(1024)(128)(4,1)}), s8[4194304]{0:T(1024)(128)(4,1)S(1)}, s32[]{:S(2)}) async-start(s8[8388608]{0:T(1024)(128)(4,1)} %bitcast.45), calls=%async_computation.5 | async-start | bytes 8388608 | tf_op jit(solution)/shard_map/while/body/eval_jaxpr/cond
  416.8 2.6 slice-start.3
  431.6 6.7 %collective-permute-start = (bf16[48,2048]{1,0:T(8,128)(2,1)S(1)}, bf16[48,2048]{1,0:T(8,128)(2,1)S(1)}, u32[]{:S(2)}, u32[]{:S(2)}) collective-permute-start(bf16[48,2048]{1,0:T(8,128)(2,1)S(1)} %add_convert_fusion.2), channel_id=1, source_target_pairs={{192,0},{0,64},{64,128},{128,192},{193,1},{1,65},{65,129},{129,193... | collective-permute-start | bytes 589832 | tf_op jit(solution)/shard_map/while/body/eval_jaxpr/ppermute | solution.py:25
  446.2 5.4 slice-start
  446.4 5.7 %slice-start.1 = ((s8[8388608]{0:T(1024)(128)(4,1)}), s8[4194304]{0:T(1024)(128)(4,1)S(1)}, s32[]{:S(2)}) async-start(s8[8388608]{0:T(1024)(128)(4,1)} %bitcast.43), calls=%async_computation.4 | async-start | bytes 8388608 | tf_op jit(solution)/shard_map/while/body/eval_jaxpr/cond
  446.4 8.3 %slice-start.2 = ((s8[8388608]{0:T(1024)(128)(4,1)}), s8[4194304]{0:T(1024)(128)(4,1)S(1)}, s32[]{:S(2)}) async-start(s8[8388608]{0:T(1024)(128)(4,1)} %bitcast.45), calls=%async_computation.5 | async-start | bytes 8388608 | tf_op jit(solution)/shard_map/while/body/eval_jaxpr/cond
  452.1 2.6 slice-start.3
  468.0 7.4 %collective-permute-start = (bf16[48,2048]{1,0:T(8,128)(2,1)S(1)}, bf16[48,2048]{1,0:T(8,128)(2,1)S(1)}, u32[]{:S(2)}, u32[]{:S(2)}) collective-permute-start(bf16[48,2048]{1,0:T(8,128)(2,1)S(1)} %add_convert_fusion.2), channel_id=1, source_target_pairs={{192,0},{0,64},{64,128},{128,192},{193,1},{1,65},{65,129},{129,193... | collective-permute-start | bytes 589832 | tf_op jit(solution)/shard_map/while/body/eval_jaxpr/ppermute | solution.py:25
  488.7 9.4 %collective-permute-start = (bf16[48,2048]{1,0:T(8,128)(2,1)S(1)}, bf16[48,2048]{1,0:T(8,128)(2,1)S(1)}, u32[]{:S(2)}, u32[]{:S(2)}) collective-permute-start(bf16[48,2048]{1,0:T(8,128)(2,1)S(1)} %add_convert_fusion.2), channel_id=1, source_target_pairs={{192,0},{0,64},{64,128},{128,192},{193,1},{1,65},{65,129},{129,193... | collective-permute-start | bytes 589832 | tf_op jit(solution)/shard_map/while/body/eval_jaxpr/ppermute | solution.py:25
Sparse Core Ops, SparseCore 0:
  10.7 186.3 all-gather.1
Sparse Core Ops, SparseCore 1:
  21.8 48.7 all-reduce.1
where the time goes:
time: 545 us; the launch traced here: 544 us
  waiting for transfers between devices  226 us (41%)
  blocking collectives  148 us (27%)
  matrix products  55.3 us (10%)
  local copies, waits for them, and re-layouts  44.1 us (8%)
  starting transfers between devices  25.6 us (5%)
  other arithmetic  16.8 us (3%)
  between operations  14.9 us (3%)
  loops' own time  12.9 us (2%)
    all_gather x1, waiting for transfers between devices, side_by_side(): out = lax.all_gather(both, axis, axis=dim, tiled=True)  175 us
    all_gather x9, blocking collectives, turn(): features = lax.all_gather(hidden, 'tp', axis=1, tiled=True)  60.4 us
    ppermute x9, waiting for transfers between devices, from_behind(): return lax.ppermute(block, axis, route)  50.9 us
    all_gather x9, blocking collectives, turn(): every_head = lax.all_gather(heads_out, 'tp', axis=1, tiled=True)  50.7 us
    ppermute x9, starting transfers between devices, from_behind(): return lax.ppermute(block, axis, route)  25.6 us
    all_to_all x1, blocking collectives, copy_for_each(): return lax.all_to_all(copies, axis, split_axis=0, concat_axis=0, tiled=True)  23.4 us
    dot_general x4, matrix products, attend(): jnp.dot(normed, query_proj, preferred_element_type=jnp.float32)  20.6 us
    dot_general x4, matrix products, turn(): jnp.dot(every_head, out_proj, preferred_element_type=jnp.float32)  19.8 us
  transfers between devices with their start and end apart: 11, of which 8 were waited for; matrix products, arithmetic and copies ran while one was open for 7% of the time, Pallas kernels for 0%

commit v1 on v0

--- a/solution.py
+++ b/solution.py
@@ -129,7 +129,9 @@
         memory = jnp.where(segment == 0, mem_init, earlier)
         hidden = jnp.where(phase_index == 0, jnp.concatenate([memory, tokens], 0), incoming)
         length = seg_lengths[document, segment]
-        features = lax.all_gather(hidden, "tp", axis=1, tiled=True)
+        features = jnp.concatenate(
+            lax.all_to_all(jnp.stack([hidden] * lax.axis_size("tp")), "tp", 0, 0), axis=1
+        )
         heads_out = lax.cond(
             active,
             lambda: attend(features, length, query_proj, key_proj, value_proj, norm_row),

time: 545 us -> 584 us (1.072)
  blocking collectives: 148 us -> 88.4 us
  starting transfers between devices: 25.6 us -> 74.7 us
  waiting for transfers between devices: 226 us -> 264 us
  other arithmetic: 16.8 us -> 27 us
    all_gather x9 -> x0, blocking collectives: 60.4 us -> none  [turn(): features = lax.all_gather(hidden, 'tp', axis=1, tiled=True)]
    all_to_all x0 -> x9, starting transfers between devices: none -> 47.3 us  [turn(): lax.all_to_all(jnp.stack([hidden] * lax.axis_size('tp')), 'tp', 0, 0)]
    all_to_all x0 -> x9, waiting for transfers between devices: none -> 19.1 us  [turn(): lax.all_to_all(jnp.stack([hidden] * lax.axis_size('tp')), 'tp', 0, 0)]
    ppermute x9, waiting for transfers between devices: 50.9 us -> 69.3 us  [from_behind(): return lax.ppermute(block, axis, route)]
    another operation x0 -> x18, other arithmetic: none -> 7.41 us  [turn(): jnp.stack([hidden] * lax.axis_size('tp'))]
  transfers between devices with their start and end apart: 11 -> 20, of which waited for: 8 -> 19; matrix products, arithmetic and copies ran while one was open for 7% -> 7% of each run, Pallas kernels for 0% -> 0%
where the time goes in v1:
time: 584 us; the launch traced here: 582 us
  waiting for transfers between devices  264 us (45%)
  blocking collectives  88.4 us (15%)
  starting transfers between devices  74.7 us (13%)
  matrix products  54.6 us (9%)
  local copies, waits for them, and re-layouts  46.4 us (8%)
  other arithmetic  27 us (5%)
  between operations  14.9 us (3%)
  loops' own time  12.1 us (2%)
    all_gather x1, waiting for transfers between devices, side_by_side(): out = lax.all_gather(both, axis, axis=dim, tiled=True)  175 us
    ppermute x9, waiting for transfers between devices, from_behind(): return lax.ppermute(block, axis, route)  69.3 us
    all_gather x9, blocking collectives, turn(): every_head = lax.all_gather(heads_out, 'tp', axis=1, tiled=True)  50.2 us
    all_to_all x9, starting transfers between devices, turn(): lax.all_to_all(jnp.stack([hidden] * lax.axis_size('tp')), 'tp', 0, 0)  47.3 us
    ppermute x9, starting transfers between devices, from_behind(): return lax.ppermute(block, axis, route)  27.4 us
    all_to_all x1, blocking collectives, copy_for_each(): return lax.all_to_all(copies, axis, split_axis=0, concat_axis=0, tiled=True)  23.4 us
    dot_general x4, matrix products, attend(): jnp.dot(normed, query_proj, preferred_element_type=jnp.float32)  20.5 us
    dot_general x4, matrix products, turn(): jnp.dot(every_head, out_proj, preferred_element_type=jnp.float32)  19.8 us
  transfers between devices with their start and end apart: 20, of which 19 were waited for; matrix products, arithmetic and copies ran while one was open for 7% of the time, Pallas kernels for 0%

profile of v1, /device:TPU:6, one launch (start us, length us, event | category | flops | bytes accessed | tf_op | source)
XLA Modules:
  0.0 582.1 jit_solution(11231503142627695007)
XLA Ops:
  7.4 2.1 pad_maximum_fusion.1
  11.2 9.4 %gather_fusion = bf16[128,2048]{1,0:T(8,128)(2,1)S(1)} fusion(bf16[4096,2048]{1,0:T(8,128)(2,1)} %param.18, s32[1024]{0:T(1024)S(1)} %pad_clamp_fusion), kind=kCustom, calls=%fused_computation | custom fusion | bytes 1049088 | tf_op jit(solution)/shard_map/jit(_take)/gather | solution.py:107
  21.8 175.4 %all-gather.2.cloned.1.call-done = bf16[4096,3072]{1,0:T(8,128)(2,1)} async-done(((bf16[128,3072]{1,0:T(8,128)(2,1)}), bf16[4096,3072]{1,0:T(8,128)(2,1)}) %all-gather.2.cloned.1.call-update) | async-done | bytes 25165840 | tf_op jit(solution)/shard_map/all_gather | solution.py:18
  197.2 16.9 %fusion.20 = (bf16[4096,1024]{1,0:T(8,128)(2,1)}, bf16[4096,1024]{1,0:T(8,128)(2,1)}, bf16[4096,1024]{1,0:T(8,128)(2,1)}) fusion(bf16[4096,3072]{1,0:T(8,128)(2,1)} %all-gather.2.cloned.1.call-done), kind=kLoop, calls=%fused_computation.52 | loop fusion | bytes 50331648 | tf_op jit(solution)/shard_map/split | solution.py:19
  214.2 320.8 %while.18 = (s32[]{:T(128)}, bf16[48,2048]{1,0:T(8,128)(2,1)S(1)}, f32[2,2048]{1,0:T(2,128)S(1)}, pred[]{:T(512)}, s32[]{:T(128)}, /*index=5*/bf16[16,2048]{1,0:...) while((s32[]{:T(128)}, bf16[48,2048]{1,0:T(8,128)(2,1)S(1)}, ...), condition=%wide.region_9.10_spmd.clone, body=%wide.region_1.9_spmd.clone.sunk | while | flops 1623443072 | bytes 96115064 | solution.py:162
  216.0 4.3 all-to-all-start
  222.7 2.0 all-to-all-done
  224.7 5.3 all_gather.16
  230.4 6.4 %collective-permute-done = bf16[48,2048]{1,0:T(8,128)(2,1)S(1)} collective-permute-done((bf16[48,2048]{1,0:T(8,128)(2,1)S(1)}, bf16[48,2048]{1,0:T(8,128)(2,1)S(1)}, u32[]{:S(2)}, u32[]{:S(2)}) %collective-permute-start) | collective-permute-done | bytes 196640 | tf_op jit(solution)/shard_map/while/body/eval_jaxpr/ppermute | solution.py:25
  238.5 5.2 all-to-all-start
  246.1 1.5 all-to-all-done
  247.6 5.7 all_gather.16
  253.4 11.5 %collective-permute-start = (bf16[48,2048]{1,0:T(8,128)(2,1)S(1)}, bf16[48,2048]{1,0:T(8,128)(2,1)S(1)}, u32[]{:S(2)}, u32[]{:S(2)}) collective-permute-start(bf16[48,2048]{1,0:T(8,128)(2,1)S(1)} %add_convert_fusion.2), channel_id=1, source_target_pairs={{192,0},{0,64},{64,128},{128,192},{193,1},{1,65},{65,129},{129,193... | collective-permute-start | bytes 589832 | tf_op jit(solution)/shard_map/while/body/eval_jaxpr/ppermute | solution.py:25
  265.1 19.4 %collective-permute-done = bf16[48,2048]{1,0:T(8,128)(2,1)S(1)} collective-permute-done((bf16[48,2048]{1,0:T(8,128)(2,1)S(1)}, bf16[48,2048]{1,0:T(8,128)(2,1)S(1)}, u32[]{:S(2)}, u32[]{:S(2)}) %collective-permute-start) | collective-permute-done | bytes 196640 | tf_op jit(solution)/shard_map/while/body/eval_jaxpr/ppermute | solution.py:25
  286.4 3.5 all-to-all-start
  292.3 3.5 all-to-all-done
  295.8 11.9 %conditional.6 = (bf16[48,1024]{1,0:T(8,128)(2,1)S(1)}) conditional(s32[]{:T(128)} %convert_element_type.144, () %tuple.66, (bf16[48,2,2048]{2,0,1:T(8,128)(2,1)S(1)}, f32[1,4096]{1,0:T(1,128)S(1)}, bf16[4096,1024]{1,0:T(8,128)(2,1)}, s32[]{:T(128)}, bf16[4096,1024]{1,0:T(8,128)(2,1)}, /*index=5*/bf16[4096,1024]{1,0:T(8,128)(2,1)}) %tuple.81), branch_computations={%region_2.2_spmd, %region_3.5_spmd} | conditional | flops 1219071616 | bytes 82056752 | solution.py:135
  297.5 5.1 fusion.5
  303.3 1.6 fusion.6
  305.8 1.6 fusion.4
  307.7 5.3 all_gather.16
  313.0 4.9 conditional.7
  313.0 4.9 fusion.21
  318.3 6.7 %collective-permute-done = bf16[48,2048]{1,0:T(8,128)(2,1)S(1)} collective-permute-done((bf16[48,2048]{1,0:T(8,128)(2,1)S(1)}, bf16[48,2048]{1,0:T(8,128)(2,1)S(1)}, u32[]{:S(2)}, u32[]{:S(2)}) %collective-permute-start) | collective-permute-done | bytes 196640 | tf_op jit(solution)/shard_map/while/body/eval_jaxpr/ppermute | solution.py:25
  326.7 4.6 all-to-all-start
  335.2 11.9 %conditional.6 = (bf16[48,1024]{1,0:T(8,128)(2,1)S(1)}) conditional(s32[]{:T(128)} %convert_element_type.144, () %tuple.66, (bf16[48,2,2048]{2,0,1:T(8,128)(2,1)S(1)}, f32[1,4096]{1,0:T(1,128)S(1)}, bf16[4096,1024]{1,0:T(8,128)(2,1)}, s32[]{:T(128)}, bf16[4096,1024]{1,0:T(8,128)(2,1)}, /*index=5*/bf16[4096,1024]{1,0:T(8,128)(2,1)}) %tuple.81), branch_computations={%region_2.2_spmd, %region_3.5_spmd} | conditional | flops 1219071616 | bytes 82056752 | solution.py:135
  336.9 5.1 fusion.5
  342.6 1.6 fusion.6
  345.2 1.6 fusion.4
  347.1 5.9 %all_gather.16 = bf16[48,2048]{1,0:T(8,128)(2,1)S(1)} all-gather(bf16[48,1024]{1,0:T(8,128)(2,1)S(1)} %get-tuple-element.606), channel_id=1, replica_groups=mesh['section'=4,'tp'=2,'doc'=32] {'tp'}, dimensions={1}, use_global_device_ids=true | all-gather | bytes 294912 | tf_op jit(solution)/shard_map/while/body/eval_jaxpr/all_gather | solution.py:140
  353.0 4.9 conditional.7
  353.0 4.9 fusion.21
  358.3 6.4 %collective-permute-done = bf16[48,2048]{1,0:T(8,128)(2,1)S(1)} collective-permute-done((bf16[48,2048]{1,0:T(8,128)(2,1)S(1)}, bf16[48,2048]{1,0:T(8,128)(2,1)S(1)}, u32[]{:S(2)}, u32[]{:S(2)}) %collective-permute-start) | collective-permute-done | bytes 196640 | tf_op jit(solution)/shard_map/while/body/eval_jaxpr/ppermute | solution.py:25
  366.4 7.5 %all-to-all-start = ((bf16[2,48,2048]{2,1,0:T(8,128)(2,1)}), bf16[2,48,2048]{2,1,0:T(8,128)(2,1)S(1)}, u32[]{:S(2)}, u32[]{:S(2)}) async-start(bf16[2,48,2048]{2,1,0:T(8,128)(2,1)} %pad_maximum_fusion.3), calls=%async_computation | async-start | bytes 786432 | tf_op jit(solution)/shard_map/while/body/eval_jaxpr/all_to_all | solution.py:133
  377.8 5.3 all_gather.16
  383.2 7.8 %collective-permute-start = (bf16[48,2048]{1,0:T(8,128)(2,1)S(1)}, bf16[48,2048]{1,0:T(8,128)(2,1)S(1)}, u32[]{:S(2)}, u32[]{:S(2)}) collective-permute-start(bf16[48,2048]{1,0:T(8,128)(2,1)S(1)} %add_convert_fusion.2), channel_id=1, source_target_pairs={{192,0},{0,64},{64,128},{128,192},{193,1},{1,65},{65,129},{129,193... | collective-permute-start | bytes 589832 | tf_op jit(solution)/shard_map/while/body/eval_jaxpr/ppermute | solution.py:25
  393.8 5.2 all-to-all-start
  401.4 2.7 all-to-all-done
  404.2 6.3 %all_gather.16 = bf16[48,2048]{1,0:T(8,128)(2,1)S(1)} all-gather(bf16[48,1024]{1,0:T(8,128)(2,1)S(1)} %get-tuple-element.606), channel_id=1, replica_groups=mesh['section'=4,'tp'=2,'doc'=32] {'tp'}, dimensions={1}, use_global_device_ids=true | all-gather | bytes 294912 | tf_op jit(solution)/shard_map/while/body/eval_jaxpr/all_gather | solution.py:140
  410.9 15.7 %collective-permute-done = bf16[48,2048]{1,0:T(8,128)(2,1)S(1)} collective-permute-done((bf16[48,2048]{1,0:T(8,128)(2,1)S(1)}, bf16[48,2048]{1,0:T(8,128)(2,1)S(1)}, u32[]{:S(2)}, u32[]{:S(2)}) %collective-permute-start) | collective-permute-done | bytes 196640 | tf_op jit(solution)/shard_map/while/body/eval_jaxpr/ppermute | solution.py:25
  428.4 4.4 all-to-all-start
  435.2 3.4 all-to-all-done
  438.6 11.9 %conditional.6 = (bf16[48,1024]{1,0:T(8,128)(2,1)S(1)}) conditional(s32[]{:T(128)} %convert_element_type.144, () %tuple.66, (bf16[48,2,2048]{2,0,1:T(8,128)(2,1)S(1)}, f32[1,4096]{1,0:T(1,128)S(1)}, bf16[4096,1024]{1,0:T(8,128)(2,1)}, s32[]{:T(128)}, bf16[4096,1024]{1,0:T(8,128)(2,1)}, /*index=5*/bf16[4096,1024]{1,0:T(8,128)(2,1)}) %tuple.81), branch_computations={%region_2.2_spmd, %region_3.5_spmd} | conditional | flops 1219071616 | bytes 82056752 | solution.py:135
  440.3 5.1 fusion.5
  446.0 1.6 fusion.6
  448.6 1.6 fusion.4
  450.4 5.3 all_gather.16
  455.7 4.9 conditional.7
  455.7 4.9 fusion.21
  461.0 6.7 %collective-permute-done = bf16[48,2048]{1,0:T(8,128)(2,1)S(1)} collective-permute-done((bf16[48,2048]{1,0:T(8,128)(2,1)S(1)}, bf16[48,2048]{1,0:T(8,128)(2,1)S(1)}, u32[]{:S(2)}, u32[]{:S(2)}) %collective-permute-start) | collective-permute-done | bytes 196640 | tf_op jit(solution)/shard_map/while/body/eval_jaxpr/ppermute | solution.py:25
  469.5 4.6 all-to-all-start
  477.9 11.9 %conditional.6 = (bf16[48,1024]{1,0:T(8,128)(2,1)S(1)}) conditional(s32[]{:T(128)} %convert_element_type.144, () %tuple.66, (bf16[48,2,2048]{2,0,1:T(8,128)(2,1)S(1)}, f32[1,4096]{1,0:T(1,128)S(1)}, bf16[4096,1024]{1,0:T(8,128)(2,1)}, s32[]{:T(128)}, bf16[4096,1024]{1,0:T(8,128)(2,1)}, /*index=5*/bf16[4096,1024]{1,0:T(8,128)(2,1)}) %tuple.81), branch_computations={%region_2.2_spmd, %region_3.5_spmd} | conditional | flops 1219071616 | bytes 82056752 | solution.py:135
  479.6 5.1 fusion.5
  485.3 1.6 fusion.6
  487.9 1.6 fusion.4
  489.8 5.8 all_gather.16
  495.6 4.9 conditional.7
  495.6 4.9 fusion.21
  500.9 6.4 %collective-permute-done = bf16[48,2048]{1,0:T(8,128)(2,1)S(1)} collective-permute-done((bf16[48,2048]{1,0:T(8,128)(2,1)S(1)}, bf16[48,2048]{1,0:T(8,128)(2,1)S(1)}, u32[]{:S(2)}, u32[]{:S(2)}) %collective-permute-start) | collective-permute-done | bytes 196640 | tf_op jit(solution)/shard_map/while/body/eval_jaxpr/ppermute | solution.py:25
  509.0 8.0 %all-to-all-start = ((bf16[2,48,2048]{2,1,0:T(8,128)(2,1)}), bf16[2,48,2048]{2,1,0:T(8,128)(2,1)S(1)}, u32[]{:S(2)}, u32[]{:S(2)}) async-start(bf16[2,48,2048]{2,1,0:T(8,128)(2,1)} %pad_maximum_fusion.3), calls=%async_computation | async-start | bytes 786432 | tf_op jit(solution)/shard_map/while/body/eval_jaxpr/all_to_all | solution.py:133
  520.9 5.3 all_gather.16
  526.3 7.6 %collective-permute-start = (bf16[48,2048]{1,0:T(8,128)(2,1)S(1)}, bf16[48,2048]{1,0:T(8,128)(2,1)S(1)}, u32[]{:S(2)}, u32[]{:S(2)}) collective-permute-start(bf16[48,2048]{1,0:T(8,128)(2,1)S(1)} %add_convert_fusion.2), channel_id=1, source_target_pairs={{192,0},{0,64},{64,128},{128,192},{193,1},{1,65},{65,129},{129,193... | collective-permute-start | bytes 589832 | tf_op jit(solution)/shard_map/while/body/eval_jaxpr/ppermute | solution.py:25
  535.0 14.8 %psum.15 = f32[2,2048]{1,0:T(2,128)S(1)} all-reduce(f32[2,2048]{1,0:T(2,128)S(1)} %get-tuple-element.367), channel_id=1, replica_groups=mesh['section'=4,'tp'=2,'doc'=32] {'section'}, use_global_device_ids=true, to_apply=%region_10.11 | all-reduce | flops 4096 | bytes 32768 | tf_op jit(solution)/shard_map/psum | solution.py:164
  550.0 23.4 %all_to_all.19 = f32[32,2,2048]{2,1,0:T(2,128)S(1)} all-to-all(f32[32,2,2048]{2,1,0:T(2,128)S(1)} %broadcast_in_dim.106), channel_id=1, replica_groups=mesh['section'=4,'tp'=2,'doc'=32] {'doc'}, dimensions={0} | all-to-all | bytes 1048576 | tf_op jit(solution)/shard_map/all_to_all | solution.py:36
  (235 shorter events, 55.2 us)
Async XLA Ops:
  7.4 189.8 %all-gather.2.cloned.1.call-start = ((), (), s32[]{:S(2)}) async-start(), calls=%async_computation.3 | async-start | bytes 25952256 | tf_op jit(solution)/shard_map/all_gather | solution.py:18
  9.5 204.6 %all-reduce.2.cloned.1.call-start = ((), (), s32[]{:S(2)}) async-start(), calls=%async_computation.2 | async-start | bytes 1048576 | tf_op jit(solution)/shard_map/psum | solution.py:109
  21.7 192.4 %copy-start = (bf16[16,2048]{1,0:T(8,128)(2,1)S(1)}, bf16[16,2048]{1,0:T(8,128)(2,1)}, u32[]{:S(2)}) copy-start(bf16[16,2048]{1,0:T(8,128)(2,1)} %param.19) | copy-start | bytes 196612
  21.8 192.4 %copy-start.1 = (f32[1,4096]{1,0:T(1,128)S(1)}, f32[1,4096]{1,0:T(1,128)}, u32[]{:S(2)}) copy-start(f32[1,4096]{1,0:T(1,128)} %param.20) | copy-start | bytes 49156
  21.8 192.4 %copy-start.2 = (s32[2,2]{1,0:T(2,128)S(1)}, s32[2,2]{1,0:T(2,128)}, u32[]{:S(2)}) copy-start(s32[2,2]{1,0:T(2,128)} %param.17) | copy-start | bytes 52
  216.0 8.7 %all-to-all-start = ((bf16[2,48,2048]{2,1,0:T(8,128)(2,1)}), bf16[2,48,2048]{2,1,0:T(8,128)(2,1)S(1)}, u32[]{:S(2)}, u32[]{:S(2)}) async-start(bf16[2,48,2048]{2,1,0:T(8,128)(2,1)} %pad_maximum_fusion.3), calls=%async_computation | async-start | bytes 786432 | tf_op jit(solution)/shard_map/while/body/eval_jaxpr/all_to_all | solution.py:133
  230.1 6.7 %collective-permute-start = (bf16[48,2048]{1,0:T(8,128)(2,1)S(1)}, bf16[48,2048]{1,0:T(8,128)(2,1)S(1)}, u32[]{:S(2)}, u32[]{:S(2)}) collective-permute-start(bf16[48,2048]{1,0:T(8,128)(2,1)S(1)} %add_convert_fusion.2), channel_id=1, source_target_pairs={{192,0},{0,64},{64,128},{128,192},{193,1},{1,65},{65,129},{129,193... | collective-permute-start | bytes 589832 | tf_op jit(solution)/shard_map/while/body/eval_jaxpr/ppermute | solution.py:25
  238.5 9.1 %all-to-all-start = ((bf16[2,48,2048]{2,1,0:T(8,128)(2,1)}), bf16[2,48,2048]{2,1,0:T(8,128)(2,1)S(1)}, u32[]{:S(2)}, u32[]{:S(2)}) async-start(bf16[2,48,2048]{2,1,0:T(8,128)(2,1)} %pad_maximum_fusion.3), calls=%async_computation | async-start | bytes 786432 | tf_op jit(solution)/shard_map/while/body/eval_jaxpr/all_to_all | solution.py:133
  253.4 31.1 %collective-permute-start = (bf16[48,2048]{1,0:T(8,128)(2,1)S(1)}, bf16[48,2048]{1,0:T(8,128)(2,1)S(1)}, u32[]{:S(2)}, u32[]{:S(2)}) collective-permute-start(bf16[48,2048]{1,0:T(8,128)(2,1)S(1)} %add_convert_fusion.2), channel_id=1, source_target_pairs={{192,0},{0,64},{64,128},{128,192},{193,1},{1,65},{65,129},{129,193... | collective-permute-start | bytes 589832 | tf_op jit(solution)/shard_map/while/body/eval_jaxpr/ppermute | solution.py:25
  286.4 9.5 %all-to-all-start = ((bf16[2,48,2048]{2,1,0:T(8,128)(2,1)}), bf16[2,48,2048]{2,1,0:T(8,128)(2,1)S(1)}, u32[]{:S(2)}, u32[]{:S(2)}) async-start(bf16[2,48,2048]{2,1,0:T(8,128)(2,1)} %pad_maximum_fusion.3), calls=%async_computation | async-start | bytes 786432 | tf_op jit(solution)/shard_map/while/body/eval_jaxpr/all_to_all | solution.py:133
  297.4 5.3 slice-start
  297.5 5.7 slice-start.1
  297.5 8.2 %slice-start.2 = ((s8[8388608]{0:T(1024)(128)(4,1)}), s8[4194304]{0:T(1024)(128)(4,1)S(1)}, s32[]{:S(2)}) async-start(s8[8388608]{0:T(1024)(128)(4,1)} %bitcast.57), calls=%async_computation.6 | async-start | bytes 8388608 | tf_op jit(solution)/shard_map/while/body/eval_jaxpr/cond
  303.3 2.6 slice-start.3
  318.0 7.0 %collective-permute-start = (bf16[48,2048]{1,0:T(8,128)(2,1)S(1)}, bf16[48,2048]{1,0:T(8,128)(2,1)S(1)}, u32[]{:S(2)}, u32[]{:S(2)}) collective-permute-start(bf16[48,2048]{1,0:T(8,128)(2,1)S(1)} %add_convert_fusion.2), channel_id=1, source_target_pairs={{192,0},{0,64},{64,128},{128,192},{193,1},{1,65},{65,129},{129,193... | collective-permute-start | bytes 589832 | tf_op jit(solution)/shard_map/while/body/eval_jaxpr/ppermute | solution.py:25
  326.7 8.5 %all-to-all-start = ((bf16[2,48,2048]{2,1,0:T(8,128)(2,1)}), bf16[2,48,2048]{2,1,0:T(8,128)(2,1)S(1)}, u32[]{:S(2)}, u32[]{:S(2)}) async-start(bf16[2,48,2048]{2,1,0:T(8,128)(2,1)} %pad_maximum_fusion.3), calls=%async_computation | async-start | bytes 786432 | tf_op jit(solution)/shard_map/while/body/eval_jaxpr/all_to_all | solution.py:133
  336.7 5.3 slice-start
  336.9 5.7 slice-start.1
  336.9 8.2 %slice-start.2 = ((s8[8388608]{0:T(1024)(128)(4,1)}), s8[4194304]{0:T(1024)(128)(4,1)S(1)}, s32[]{:S(2)}) async-start(s8[8388608]{0:T(1024)(128)(4,1)} %bitcast.57), calls=%async_computation.6 | async-start | bytes 8388608 | tf_op jit(solution)/shard_map/while/body/eval_jaxpr/cond
  342.6 2.6 slice-start.3
  358.0 6.7 %collective-permute-start = (bf16[48,2048]{1,0:T(8,128)(2,1)S(1)}, bf16[48,2048]{1,0:T(8,128)(2,1)S(1)}, u32[]{:S(2)}, u32[]{:S(2)}) collective-permute-start(bf16[48,2048]{1,0:T(8,128)(2,1)S(1)} %add_convert_fusion.2), channel_id=1, source_target_pairs={{192,0},{0,64},{64,128},{128,192},{193,1},{1,65},{65,129},{129,193... | collective-permute-start | bytes 589832 | tf_op jit(solution)/shard_map/while/body/eval_jaxpr/ppermute | solution.py:25
  366.4 11.4 %all-to-all-start = ((bf16[2,48,2048]{2,1,0:T(8,128)(2,1)}), bf16[2,48,2048]{2,1,0:T(8,128)(2,1)S(1)}, u32[]{:S(2)}, u32[]{:S(2)}) async-start(bf16[2,48,2048]{2,1,0:T(8,128)(2,1)} %pad_maximum_fusion.3), calls=%async_computation | async-start | bytes 786432 | tf_op jit(solution)/shard_map/while/body/eval_jaxpr/all_to_all | solution.py:133
  383.2 8.8 %collective-permute-start = (bf16[48,2048]{1,0:T(8,128)(2,1)S(1)}, bf16[48,2048]{1,0:T(8,128)(2,1)S(1)}, u32[]{:S(2)}, u32[]{:S(2)}) collective-permute-start(bf16[48,2048]{1,0:T(8,128)(2,1)S(1)} %add_convert_fusion.2), channel_id=1, source_target_pairs={{192,0},{0,64},{64,128},{128,192},{193,1},{1,65},{65,129},{129,193... | collective-permute-start | bytes 589832 | tf_op jit(solution)/shard_map/while/body/eval_jaxpr/ppermute | solution.py:25
  393.8 10.3 %all-to-all-start = ((bf16[2,48,2048]{2,1,0:T(8,128)(2,1)}), bf16[2,48,2048]{2,1,0:T(8,128)(2,1)S(1)}, u32[]{:S(2)}, u32[]{:S(2)}) async-start(bf16[2,48,2048]{2,1,0:T(8,128)(2,1)} %pad_maximum_fusion.3), calls=%async_computation | async-start | bytes 786432 | tf_op jit(solution)/shard_map/while/body/eval_jaxpr/all_to_all | solution.py:133
  410.6 16.0 %collective-permute-start = (bf16[48,2048]{1,0:T(8,128)(2,1)S(1)}, bf16[48,2048]{1,0:T(8,128)(2,1)S(1)}, u32[]{:S(2)}, u32[]{:S(2)}) collective-permute-start(bf16[48,2048]{1,0:T(8,128)(2,1)S(1)} %add_convert_fusion.2), channel_id=1, source_target_pairs={{192,0},{0,64},{64,128},{128,192},{193,1},{1,65},{65,129},{129,193... | collective-permute-start | bytes 589832 | tf_op jit(solution)/shard_map/while/body/eval_jaxpr/ppermute | solution.py:25
  428.4 10.2 %all-to-all-start = ((bf16[2,48,2048]{2,1,0:T(8,128)(2,1)}), bf16[2,48,2048]{2,1,0:T(8,128)(2,1)S(1)}, u32[]{:S(2)}, u32[]{:S(2)}) async-start(bf16[2,48,2048]{2,1,0:T(8,128)(2,1)} %pad_maximum_fusion.3), calls=%async_computation | async-start | bytes 786432 | tf_op jit(solution)/shard_map/while/body/eval_jaxpr/all_to_all | solution.py:133
  440.1 5.3 slice-start
  440.2 5.7 slice-start.1
  440.2 8.2 %slice-start.2 = ((s8[8388608]{0:T(1024)(128)(4,1)}), s8[4194304]{0:T(1024)(128)(4,1)S(1)}, s32[]{:S(2)}) async-start(s8[8388608]{0:T(1024)(128)(4,1)} %bitcast.57), calls=%async_computation.6 | async-start | bytes 8388608 | tf_op jit(solution)/shard_map/while/body/eval_jaxpr/cond
  446.0 2.6 slice-start.3
  460.7 7.0 %collective-permute-start = (bf16[48,2048]{1,0:T(8,128)(2,1)S(1)}, bf16[48,2048]{1,0:T(8,128)(2,1)S(1)}, u32[]{:S(2)}, u32[]{:S(2)}) collective-permute-start(bf16[48,2048]{1,0:T(8,128)(2,1)S(1)} %add_convert_fusion.2), channel_id=1, source_target_pairs={{192,0},{0,64},{64,128},{128,192},{193,1},{1,65},{65,129},{129,193... | collective-permute-start | bytes 589832 | tf_op jit(solution)/shard_map/while/body/eval_jaxpr/ppermute | solution.py:25
  469.5 8.4 %all-to-all-start = ((bf16[2,48,2048]{2,1,0:T(8,128)(2,1)}), bf16[2,48,2048]{2,1,0:T(8,128)(2,1)S(1)}, u32[]{:S(2)}, u32[]{:S(2)}) async-start(bf16[2,48,2048]{2,1,0:T(8,128)(2,1)} %pad_maximum_fusion.3), calls=%async_computation | async-start | bytes 786432 | tf_op jit(solution)/shard_map/while/body/eval_jaxpr/all_to_all | solution.py:133
  479.5 5.3 slice-start
  479.6 5.7 slice-start.1
  479.6 8.2 %slice-start.2 = ((s8[8388608]{0:T(1024)(128)(4,1)}), s8[4194304]{0:T(1024)(128)(4,1)S(1)}, s32[]{:S(2)}) async-start(s8[8388608]{0:T(1024)(128)(4,1)} %bitcast.57), calls=%async_computation.6 | async-start | bytes 8388608 | tf_op jit(solution)/shard_map/while/body/eval_jaxpr/cond
  485.3 2.6 slice-start.3
  500.6 6.7 %collective-permute-start = (bf16[48,2048]{1,0:T(8,128)(2,1)S(1)}, bf16[48,2048]{1,0:T(8,128)(2,1)S(1)}, u32[]{:S(2)}, u32[]{:S(2)}) collective-permute-start(bf16[48,2048]{1,0:T(8,128)(2,1)S(1)} %add_convert_fusion.2), channel_id=1, source_target_pairs={{192,0},{0,64},{64,128},{128,192},{193,1},{1,65},{65,129},{129,193... | collective-permute-start | bytes 589832 | tf_op jit(solution)/shard_map/while/body/eval_jaxpr/ppermute | solution.py:25
  509.0 11.9 %all-to-all-start = ((bf16[2,48,2048]{2,1,0:T(8,128)(2,1)}), bf16[2,48,2048]{2,1,0:T(8,128)(2,1)S(1)}, u32[]{:S(2)}, u32[]{:S(2)}) async-start(bf16[2,48,2048]{2,1,0:T(8,128)(2,1)} %pad_maximum_fusion.3), calls=%async_computation | async-start | bytes 786432 | tf_op jit(solution)/shard_map/while/body/eval_jaxpr/all_to_all | solution.py:133
  526.3 8.7 %collective-permute-start = (bf16[48,2048]{1,0:T(8,128)(2,1)S(1)}, bf16[48,2048]{1,0:T(8,128)(2,1)S(1)}, u32[]{:S(2)}, u32[]{:S(2)}) collective-permute-start(bf16[48,2048]{1,0:T(8,128)(2,1)S(1)} %add_convert_fusion.2), channel_id=1, source_target_pairs={{192,0},{0,64},{64,128},{128,192},{193,1},{1,65},{65,129},{129,193... | collective-permute-start | bytes 589832 | tf_op jit(solution)/shard_map/while/body/eval_jaxpr/ppermute | solution.py:25
Sparse Core Ops, SparseCore 0:
  10.7 186.3 all-gather.1
Sparse Core Ops, SparseCore 1:
  21.8 48.7 all-reduce.1
